TPU v7x, 32 devices: a whole 2x2x4 slice. The times are simulated.
32 devices in a mesh: dp: 8 (over y, x, core), tensor: 4 (over z).
Axes of the slice: x: 2, y: 2, z: 4, core: 2. Of those that a mesh axis runs over, the one named last changes fastest.
Arguments:
- tokens: bfloat16 [16384, 1024], P(('dp', 'tensor')), may hold values from -6 to 6
- cotangent: bfloat16 [16384, 1024], P(('dp', 'tensor')), may hold values from -6 to 6
- lengths: int32 [8, 3], P('dp'), may hold values from 1 to 1024, 1920 in all within a row
- token_order: int32 [16384], P(('dp', 'tensor')), may hold values from 0 to 16383, as said below
- token_return: int32 [16384], P(('dp', 'tensor')), may hold values from 0 to 16383, as said below
- w_mix: float32 [1024, 8, 768], P('dp', 'tensor'), may hold values from -0.1875 to 0.1875
- w_ba: float32 [1024, 8, 2], P('dp', 'tensor'), may hold values from -0.1875 to 0.1875
- conv_w: float32 [512, 8, 4], P('dp', 'tensor'), may hold values from -3 to 3
- w_out: float32 [1024, 8, 256], P('dp', 'tensor'), may hold values from -0.1875 to 0.1875
- w_gate_up: float32 [1024, 2, 2816], P('dp', None, 'tensor'), may hold values from -0.1875 to 0.1875
- w_down: float32 [1024, 2816], P('dp', 'tensor'), may hold values from -0.15625 to 0.15625
- gain_attn: float32 [1024], replicated, may hold values from 0.25 to 1.75
- gain_ffn: float32 [1024], replicated, may hold values from 0.25 to 1.75
- gain_out: float32 [256], replicated, may hold values from 0.25 to 1.75
- decay_log: float32 [8], replicated, may hold values from -8 to -3.5
- decay_bias: float32 [8], replicated, may hold values from -1 to 1
Outputs:
- layer_out: bfloat16 [16384, 1024], P(('dp', 'tensor'))
- input_grad: bfloat16 [16384, 1024], P(('dp', 'tensor'))
- grad_w_mix: float32 [1024, 8, 768], P('dp', 'tensor')
- grad_w_ba: float32 [1024, 8, 2], P('dp', 'tensor')
- grad_conv_w: float32 [512, 8, 4], P('dp', 'tensor')
- grad_w_out: float32 [1024, 8, 256], P('dp', 'tensor')
- grad_w_gate_up: float32 [1024, 2, 2816], P('dp', None, 'tensor')
- grad_w_down: float32 [1024, 2816], P('dp', 'tensor')
- grad_gain_attn: float32 [1024], replicated
- grad_gain_ffn: float32 [1024], replicated
- grad_gain_out: float32 [256], replicated
- grad_decay_log: float32 [8], replicated
- grad_decay_bias: float32 [8], replicated
Inputs may be any that keep to these rules, and one draw needn't show every extreme that they name: `lengths`: each row sums to 1920, and its largest entry is 1024. `token_order`: a permutation. Writing a row as 2048 * g + 512 * s + i with 0 <= i < 512, packed row and given row have the same s, and for every g and g' exactly 64 packed rows of group g' with a given s take given rows of group g. `token_return`: the inverse permutation of token_order.
All inputs are finite; a program needn't handle non-finite values.
Results may differ from a plain program's by a relative error of at most 0.015.
The roundings to bfloat16 on the way count: a program that leaves them out, or rounds other values in their place, can miss the bound.
Values may be sent and summed in bfloat16 or wider, within the bound.
No kernel may reach another device: no remote copies, remote signals or barrier semaphores. Data moves between devices by JAX's collectives and lax.ppermute only.
A program may use at most 256 MiB of HBM per device.

v0:
```python
import jax
import jax.numpy as jnp
from jax import lax
from jax.sharding import PartitionSpec as P

DK = 128
DV = 256
SPAN = 64
SEQS = 3
highest_precision = lax.Precision.HIGHEST
epsilon = 1e-06


def rms_scale(values):
    return lax.rsqrt(jnp.mean(values * values, axis=-1, keepdims=True) + epsilon)


def norm_rows(values, gain):
    return values * rms_scale(values) * gain


def segments(length_row, group_rows):
    seq_ends = jnp.cumsum(length_row)
    positions = jnp.arange(group_rows, dtype=jnp.int32)
    return jnp.sum((positions[:, None] >= seq_ends[None, :]).astype(jnp.int32), axis=1)


def short_conv(inputs, weights, segment_ids):
    row_count = inputs.shape[0]
    running = inputs * jnp.transpose(weights[:, :, 0])[None]
    for offset in range(1, weights.shape[2]):
        shifted = jnp.concatenate(
            [jnp.zeros((offset,) + inputs.shape[1:], inputs.dtype), inputs[: row_count - offset]],
            axis=0,
        )
        earlier = jnp.concatenate(
            [jnp.full((offset,), -1, jnp.int32), segment_ids[: row_count - offset]]
        )
        running = (
            running
            + jnp.where((earlier == segment_ids)[:, None, None], shifted, 0.0)
            * jnp.transpose(weights[:, :, offset])[None]
        )
    return running


def mixer_core(
    projected, small_proj, conv_weights, decay_rate, decay_shift, gain_norm, segment_ids, recurrence
):
    conv_width = 2 * DK + DV
    active = jax.nn.silu(short_conv(projected[:, :, :conv_width], conv_weights, segment_ids))
    query_vec = active[:, :, :DK]
    key_vec = active[:, :, DK : 2 * DK]
    value_vec = active[:, :, 2 * DK :]
    query_vec = (
        query_vec
        * lax.rsqrt(jnp.sum(query_vec * query_vec, axis=-1, keepdims=True) + epsilon)
        * DK ** (-0.5)
    )
    key_vec = key_vec * lax.rsqrt(jnp.sum(key_vec * key_vec, axis=-1, keepdims=True) + epsilon)
    beta_gate = jax.nn.sigmoid(small_proj[:, :, 0])
    log_decay = -jnp.exp(decay_rate)[None, :] * jax.nn.softplus(
        small_proj[:, :, 1] + decay_shift[None, :]
    )
    result = recurrence(query_vec, key_vec, value_vec, beta_gate, log_decay, segment_ids)
    normed = result * rms_scale(result) * gain_norm
    gated_out = normed * jax.nn.silu(projected[:, :, conv_width:])
    return gated_out * (segment_ids < SEQS).astype(gated_out.dtype)[:, None, None]


def delta_blocks(query_vec, key_vec, value_vec, beta_gate, log_decay, segment_ids):
    total_rows = query_vec.shape[0]
    block_count = total_rows // SPAN
    before_ids = jnp.concatenate([jnp.full((1,), -1, jnp.int32), segment_ids[:-1]])[::SPAN]
    lower_tri = jnp.tril(jnp.ones((SPAN, SPAN), dtype=bool))
    strict_tri = jnp.tril(jnp.ones((SPAN, SPAN), dtype=bool), -1)

    def split_rows(array):
        return array.reshape((block_count, SPAN) + array.shape[1:])

    def one_block(recurrent_matrix, pieces):
        query_rows, block_of_keys, values_block, beta_rows, decays, seg_block, before_id = pieces
        cumulative = jnp.cumsum(decays, axis=0)
        same_seg = seg_block[:, None] == seg_block[None, :]
        log_gap = cumulative[:, None, :] - cumulative[None, :, :]
        pairwise_decay = jnp.where(
            (same_seg & lower_tri)[:, :, None], jnp.exp(jnp.minimum(log_gap, 0.0)), 0.0
        )
        pairwise_decay = jnp.transpose(pairwise_decay, (2, 0, 1))
        carry_scale = jnp.transpose(
            jnp.where((seg_block == before_id)[:, None], jnp.exp(cumulative), 0.0)
        )
        beta_cols = jnp.transpose(beta_rows)[:, :, None]
        key_key = jnp.einsum(
            "ihk,jhk->hij", block_of_keys, block_of_keys, precision=highest_precision
        )
        lower_part = jnp.where(strict_tri[None], pairwise_decay * key_key, 0.0) * beta_cols
        key_state_product = jnp.einsum(
            "grm,rmj->rgj", block_of_keys, recurrent_matrix, precision=highest_precision
        )
        right_side = beta_cols * (
            jnp.transpose(values_block, (1, 0, 2)) - carry_scale[:, :, None] * key_state_product
        )
        delta_update_rows = jax.scipy.linalg.solve_triangular(
            lower_part, right_side, lower=True, unit_diagonal=True
        )
        query_state_product = jnp.einsum(
            "grm,rmj->rgj", query_rows, recurrent_matrix, precision=highest_precision
        )
        query_key = jnp.einsum(
            "ihk,jhk->hij", query_rows, block_of_keys, precision=highest_precision
        )
        outputs = carry_scale[:, :, None] * query_state_product + jnp.einsum(
            "hij,hjv->hiv",
            query_key * pairwise_decay,
            delta_update_rows,
            precision=highest_precision,
        )
        new_state = carry_scale[:, -1][:, None, None] * recurrent_matrix + jnp.einsum(
            "tdx,dt,dtg->dxg",
            block_of_keys,
            pairwise_decay[:, -1, :],
            delta_update_rows,
            precision=highest_precision,
        )
        return (new_state, jnp.transpose(outputs, (1, 0, 2)))

    block_items = (
        split_rows(query_vec),
        split_rows(key_vec),
        split_rows(value_vec),
        split_rows(beta_gate),
        split_rows(log_decay),
        split_rows(segment_ids),
        before_ids,
    )
    initial = jnp.zeros((query_vec.shape[1], DK, DV), query_vec.dtype)
    outputs = lax.scan(jax.checkpoint(one_block), initial, block_items)[1]
    return outputs.reshape(total_rows, query_vec.shape[1], DV)


def body(
    tokens,
    cotangent,
    lengths,
    token_order,
    token_return,
    w_mix,
    w_ba,
    conv_w,
    w_out,
    w_gate_up,
    w_down,
    gain_attn,
    gain_ffn,
    gain_out,
    decay_log,
    decay_bias,
):
    groups = lax.axis_size("dp")
    splits = lax.axis_size("tensor")
    local_rows = tokens.shape[0]
    model_width = tokens.shape[1]
    group_rows = local_rows * splits
    per_peer = local_rows // groups
    send_key = token_return // group_rows * local_rows + token_return % local_rows
    send_order = jnp.argsort(send_key)
    recv_key = token_order // group_rows * local_rows + jnp.arange(local_rows, dtype=jnp.int32)
    recv_order = jnp.argsort(recv_key)
    recv_place = jnp.argsort(recv_order)
    arrived = (
        lax.all_to_all(
            tokens[send_order].reshape(groups, per_peer, model_width),
            "dp",
            split_axis=0,
            concat_axis=0,
            tiled=True,
        ),
        lax.all_to_all(
            cotangent[send_order].reshape(groups, per_peer, model_width),
            "dp",
            split_axis=0,
            concat_axis=0,
            tiled=True,
        ),
    )
    packed_in = arrived[0].reshape(local_rows, model_width)[recv_place]
    packed_grad = arrived[1].reshape(local_rows, model_width)[recv_place]
    segment_ids = segments(lengths[0], group_rows)
    row_mask = (segment_ids < SEQS).astype(jnp.float32)[:, None]
    mix_all, small_all, conv_all, out_all, ffn_all, down_all = (
        lax.all_gather(w_mix.astype(jnp.bfloat16), "dp", axis=0, tiled=True),
        lax.all_gather(w_ba.astype(jnp.bfloat16), "dp", axis=0, tiled=True),
        lax.all_gather(conv_w.astype(jnp.bfloat16), "dp", axis=0, tiled=True),
        lax.all_gather(w_out.astype(jnp.bfloat16), "dp", axis=0, tiled=True),
        lax.all_gather(w_gate_up.astype(jnp.bfloat16), "dp", axis=0, tiled=True),
        lax.all_gather(w_down.astype(jnp.bfloat16), "dp", axis=0, tiled=True),
    )
    input_f32 = packed_in.astype(jnp.float32)
    normed_f32, norm_attn_back = jax.vjp(norm_rows, input_f32, gain_attn)
    normed_all, grad_all = (
        lax.all_gather(normed_f32.astype(jnp.bfloat16), "tensor", axis=0, tiled=True),
        lax.all_gather(packed_grad, "tensor", axis=0, tiled=True),
    )
    projected = jnp.einsum("td,dhp->thp", normed_all, mix_all, preferred_element_type=jnp.float32)
    small_proj = jnp.einsum(
        "td,dhc->thc", normed_all, small_all, preferred_element_type=jnp.float32
    )
    heads_here = mix_all.shape[1]
    head_start = lax.axis_index("tensor") * heads_here
    rate_here = lax.dynamic_slice_in_dim(decay_log, head_start, heads_here)
    shift_here = lax.dynamic_slice_in_dim(decay_bias, head_start, heads_here)

    def core_pass(proj_in, small_in, conv_in, rate_in, shift_in, gain_in):
        return mixer_core(
            proj_in, small_in, conv_in, rate_in, shift_in, gain_in, segment_ids, delta_blocks
        )

    gated_f32, core_back = jax.vjp(
        core_pass,
        projected,
        small_proj,
        conv_all.astype(jnp.float32),
        rate_here,
        shift_here,
        gain_out,
    )
    gated_out = gated_f32.astype(jnp.bfloat16)
    middle = input_f32 + lax.psum_scatter(
        jnp.einsum("thv,dhv->td", gated_out, out_all, preferred_element_type=jnp.float32),
        "tensor",
        scatter_dimension=0,
        tiled=True,
    )
    normed_mid_f32, norm_ffn_back = jax.vjp(norm_rows, middle, gain_ffn)
    normed_mid_all = lax.all_gather(
        normed_mid_f32.astype(jnp.bfloat16), "tensor", axis=0, tiled=True
    )
    gate_up = jnp.einsum("td,dcf->tcf", normed_mid_all, ffn_all, preferred_element_type=jnp.float32)

    def activate(pair_in):
        return jax.nn.silu(pair_in[:, 0]) * pair_in[:, 1] * row_mask

    hidden_f32, act_back = jax.vjp(activate, gate_up)
    hidden = hidden_f32.astype(jnp.bfloat16)
    layer_rows = (
        middle
        + lax.psum_scatter(
            jnp.einsum("tf,df->td", hidden, down_all, preferred_element_type=jnp.float32).astype(
                jnp.bfloat16
            ),
            "tensor",
            scatter_dimension=0,
            tiled=True,
        ).astype(jnp.float32)
    ).astype(jnp.bfloat16)
    grad_down = jnp.einsum("td,tf->df", grad_all, hidden, preferred_element_type=jnp.float32)
    grad_hidden = jnp.einsum("td,df->tf", grad_all, down_all, preferred_element_type=jnp.float32)
    grad_pair = act_back(grad_hidden)[0].astype(jnp.bfloat16)
    grad_ffn_w = jnp.einsum(
        "td,tcf->dcf", normed_mid_all, grad_pair, preferred_element_type=jnp.float32
    )
    grad_mid_norm, grad_gain_ffn = norm_ffn_back(
        lax.psum_scatter(
            jnp.einsum("tcf,dcf->td", grad_pair, ffn_all, preferred_element_type=jnp.float32),
            "tensor",
            scatter_dimension=0,
            tiled=True,
        )
    )
    grad_middle = packed_grad.astype(jnp.float32) + grad_mid_norm
    grad_middle_all = lax.all_gather(grad_middle.astype(jnp.bfloat16), "tensor", axis=0, tiled=True)
    grad_out_w = jnp.einsum(
        "thv,td->dhv", gated_out, grad_middle_all, preferred_element_type=jnp.float32
    )
    grad_gated = jnp.einsum(
        "td,dhv->thv", grad_middle_all, out_all, preferred_element_type=jnp.float32
    )
    grad_proj, grad_small, grad_conv, grad_rate, grad_shift, grad_gain_out = core_back(grad_gated)
    grad_proj = grad_proj.astype(jnp.bfloat16)
    grad_small = grad_small.astype(jnp.bfloat16)
    grad_mix_w = jnp.einsum(
        "td,thp->dhp", normed_all, grad_proj, preferred_element_type=jnp.float32
    )
    grad_small_w = jnp.einsum(
        "td,thc->dhc", normed_all, grad_small, preferred_element_type=jnp.float32
    )
    grad_normed = lax.psum_scatter(
        (
            jnp.einsum("thp,dhp->td", grad_proj, mix_all, preferred_element_type=jnp.float32)
            + jnp.einsum("thc,dhc->td", grad_small, small_all, preferred_element_type=jnp.float32)
        ).astype(jnp.bfloat16),
        "tensor",
        scatter_dimension=0,
        tiled=True,
    ).astype(jnp.float32)
    grad_input_norm, grad_gain_attn = norm_attn_back(grad_normed)
    grad_rows = (grad_middle + grad_input_norm).astype(jnp.bfloat16)
    owned = (
        lax.psum_scatter(grad_mix_w, "dp", scatter_dimension=0, tiled=True),
        lax.psum_scatter(grad_small_w, "dp", scatter_dimension=0, tiled=True),
        lax.psum_scatter(grad_conv, "dp", scatter_dimension=0, tiled=True),
        lax.psum_scatter(grad_out_w, "dp", scatter_dimension=0, tiled=True),
        lax.psum_scatter(grad_ffn_w, "dp", scatter_dimension=0, tiled=True),
        lax.psum_scatter(grad_down, "dp", scatter_dimension=0, tiled=True),
    )
    head_total = decay_log.shape[0]
    rate_full = lax.dynamic_update_slice_in_dim(
        jnp.zeros((head_total,), jnp.float32), grad_rate, head_start, 0
    )
    shift_full = lax.dynamic_update_slice_in_dim(
        jnp.zeros((head_total,), jnp.float32), grad_shift, head_start, 0
    )
    small_sums = lax.psum(
        (grad_gain_attn, grad_gain_ffn, grad_gain_out, rate_full, shift_full), ("dp", "tensor")
    )
    returned = (
        lax.all_to_all(
            layer_rows[recv_order].reshape(groups, per_peer, model_width),
            "dp",
            split_axis=0,
            concat_axis=0,
            tiled=True,
        ),
        lax.all_to_all(
            grad_rows[recv_order].reshape(groups, per_peer, model_width),
            "dp",
            split_axis=0,
            concat_axis=0,
            tiled=True,
        ),
    )
    back_place = jnp.argsort(send_order)
    layer_out = returned[0].reshape(local_rows, model_width)[back_place]
    input_grad = returned[1].reshape(local_rows, model_width)[back_place]
    return (
        layer_out,
        input_grad,
        owned[0],
        owned[1],
        owned[2],
        owned[3],
        owned[4],
        owned[5],
        small_sums[0],
        small_sums[1],
        small_sums[2],
        small_sums[3],
        small_sums[4],
    )


def solution(mesh):
    placed = (
        P(("dp", "tensor"), None),
        P(("dp", "tensor"), None),
        P("dp", None),
        P(("dp", "tensor")),
        P(("dp", "tensor")),
        P("dp", "tensor", None),
        P("dp", "tensor", None),
        P("dp", "tensor", None),
        P("dp", "tensor", None),
        P("dp", None, "tensor"),
        P("dp", "tensor"),
        P(),
        P(),
        P(),
        P(),
        P(),
    )
    return jax.shard_map(
        body,
        mesh=mesh,
        in_specs=placed,
        out_specs=(
            P(("dp", "tensor"), None),
            P(("dp", "tensor"), None),
            P("dp", "tensor", None),
            P("dp", "tensor", None),
            P("dp", "tensor", None),
            P("dp", "tensor", None),
            P("dp", None, "tensor"),
            P("dp", "tensor"),
            P(),
            P(),
            P(),
            P(),
            P(),
        ),
        check_vma=False,
    )
```

profile of v0, /device:TPU:0, one launch (start us, length us, event | category | flops | bytes accessed | tf_op | source)
XLA Modules:
  0.0 3141.6 jit_solution(17922218729090918797)
XLA Ops:
  68.7 65.3 %all-gather.10.cloned.1.call-done = bf16[2048,1024]{1,0:T(8,128)(2,1)} async-done(((bf16[512,1024]{1,0:T(8,128)(2,1)}), bf16[2048,1024]{1,0:T(8,128)(2,1)}) %all-gather.10.cloned.1.call-update) | async-done | bytes 4194320 | tf_op jit(solution)/shard_map/all_gather | solution.py:202
  157.5 14.5 fusion.136
  192.0 641.0 %while.41 = (s32[]{:T(128)}, f32[2,128,256]{2,1,0:T(8,128)S(1)}, f32[32,64,2,256]{3,1,2,0:T(8,128)}, f32[32,2,128,256]{3,2,1,0:T(8,128)}, s32[32,64]{1,0:T(8,128...) while((s32[]{:T(128)}, f32[2,128,256]{2,1,0:T(8,128)S(1)}, ...), condition=%wide.region_10.12_spmd.clone, body=%wide.region_8.11_spmd.clone.sunk | while | flops 227238144 | bytes 3428001 | solution.py:138
  853.2 141.1 %reduce-scatter.15.cloned.1.call-done = f32[512,1024]{1,0:T(8,128)} async-done(((f32[2048,1024]{1,0:T(8,128)}), f32[512,1024]{1,0:T(8,128)}) %reduce-scatter.15.cloned.1.call-update) | async-done | bytes 2097168 | tf_op jit(solution)/shard_map/reduce_scatter | solution.py:229
  1002.0 21.4 all_to_all.20
  1036.6 82.8 %all-gather.16.cloned.1.call-done = bf16[2048,1024]{1,0:T(8,128)(2,1)} async-done(((bf16[512,1024]{1,0:T(8,128)(2,1)}), bf16[2048,1024]{1,0:T(8,128)(2,1)}) %all-gather.16.cloned.1.call-update) | async-done | bytes 4194320 | tf_op jit(solution)/shard_map/all_gather | solution.py:236
  1119.4 12.0 fusion.149
  1131.5 14.3 all-gather.20.cloned.1.call-done
  1145.7 82.4 %all-gather.24.cloned.1.call-done = bf16[2048,1024]{1,0:T(8,128)(2,1)} async-done(((bf16[512,1024]{1,0:T(8,128)(2,1)}), bf16[2048,1024]{1,0:T(8,128)(2,1)}) %all-gather.24.cloned.1.call-update) | async-done | bytes 4194320 | tf_op jit(solution)/shard_map/all_gather | solution.py:203
  1253.0 143.1 %reduce-scatter.19.cloned.1.call-done = f32[512,1024]{1,0:T(8,128)} async-done(((f32[2048,1024]{1,0:T(8,128)}), f32[512,1024]{1,0:T(8,128)}) %reduce-scatter.19.cloned.1.call-update) | async-done | bytes 2097168 | tf_op jit(solution)/shard_map/reduce_scatter | solution.py:264
  1402.6 79.7 %all-gather.22.cloned.1.call-done = bf16[2048,1024]{1,0:T(8,128)(2,1)} async-done(((bf16[512,1024]{1,0:T(8,128)(2,1)}), bf16[2048,1024]{1,0:T(8,128)(2,1)}) %all-gather.22.cloned.1.call-update) | async-done | bytes 4194320 | tf_op jit(solution)/shard_map/all_gather | solution.py:272
  1502.3 1108.9 %while.42 = (s32[]{:T(128)}, f32[2,128,256]{2,1,0:T(8,128)}, f32[32,64,2,128]{3,1,0,2:T(8,128)}, f32[32,64,2,128]{3,1,0,2:T(8,128)S(1)}, f32[32,64,2,256]{3,1,0,...) while((s32[]{:T(128)}, f32[2,128,256]{2,1,0:T(8,128)}, ...), condition=%wide.region_29.31_spmd.clone, body=%wide.region_19.30_spmd.clone.sunk | while | flops 612151424 | bytes 10787363 | solution.py:138
  2625.6 16.1 multiply_reduce_fusion.8
  2653.5 13.7 multiply_add_fusion
  2700.7 12.9 fusion.152
  2734.2 21.6 reduce-scatter.21.cloned.1.call-done
  2758.0 77.4 %reduce-scatter.17.cloned.1.call-done = bf16[512,1024]{1,0:T(8,128)(2,1)} async-done(((bf16[2048,1024]{1,0:T(8,128)(2,1)}), bf16[512,1024]{1,0:T(8,128)(2,1)}) %reduce-scatter.17.cloned.1.call-update) | async-done | bytes 1048592 | tf_op jit(solution)/shard_map/reduce_scatter | solution.py:248
  2848.5 12.6 all-to-all-done.3
  2875.0 37.1 %reduce-scatter.31.cloned.1.call-done = f32[128,4]{1,0:T(8,128)} async-done(((f32[1024,4]{1,0:T(8,128)}), f32[128,4]{1,0:T(8,128)}) %reduce-scatter.31.cloned.1.call-update) | async-done | bytes 2064
  2913.6 42.9 %reduce-scatter.25.cloned.1.call-done = f32[128,2,256]{2,0,1:T(8,128)} async-done(((f32[1024,2,256]{2,0,1:T(8,128)}), f32[128,2,256]{2,0,1:T(8,128)}) %reduce-scatter.25.cloned.1.call-update) | async-done | bytes 262160 | tf_op jit(solution)/shard_map/reduce_scatter | solution.py:303
  2958.3 39.9 %all-reduce.23 = (f32[1024]{0:T(1024)}, f32[1024]{0:T(1024)}, f32[256]{0:T(256)}, f32[8]{0:T(128)}, f32[8]{0:T(128)}) all-reduce(f32[1024]{0:T(1024)S(1)} %get-tuple-element.900, f32[1024]{0:T(1024)S(1)} %copy-done.65, f32[256]{0:T(256)S(1)} %copy-done.85, ...), channel_id=1, replica_groups=mesh['dp'=8,'tensor'=4] {'dp','tensor'}, use_global_device_ids=true, to_apply=%region_45.47 | all-reduce | flops 2320 | bytes 18560 | tf_op jit(solution)/shard_map/psum | solution.py:314
  3003.8 18.7 reduce-scatter.23.cloned.1.call-done
  3025.1 46.1 %reduce-scatter.29.cloned.1.call-done = f32[128,704]{0,1:T(8,128)} async-done(((f32[1024,704]{0,1:T(8,128)}), f32[128,704]{0,1:T(8,128)}) %reduce-scatter.29.cloned.1.call-update) | async-done | bytes 360464 | tf_op jit(solution)/shard_map/reduce_scatter | solution.py:305
  3071.2 63.3 %reduce-scatter.27.cloned.1.call-done = f32[128,2,704]{0,2,1:T(8,128)} async-done(((f32[1024,2,704]{0,2,1:T(8,128)}), f32[128,2,704]{0,2,1:T(8,128)}) %reduce-scatter.27.cloned.1.call-update) | async-done | bytes 720912 | tf_op jit(solution)/shard_map/reduce_scatter | solution.py:304
  (2967 shorter events, 2057.8 us)
Async XLA Ops:
  7.2 61.5 %all-gather.12.cloned.1.call-start = ((), (), s32[]{:S(2)}) async-start(), calls=%async_computation.15 | async-start | bytes 3538944 | tf_op jit(solution)/shard_map/all_gather | solution.py:192
  17.1 22.7 all-to-all-start
  22.3 111.7 %all-gather.10.cloned.1.call-start = ((), (), s32[]{:S(2)}) async-start(), calls=%async_computation.14 | async-start | bytes 5242880 | tf_op jit(solution)/shard_map/all_gather | solution.py:202
  43.6 800.0 %all-gather.14.cloned.1.call-start = ((), (), s32[]{:S(2)}) async-start(), calls=%async_computation.16 | async-start | bytes 1179648 | tf_op jit(solution)/shard_map/all_gather | solution.py:195
  44.4 949.9 %reduce-scatter.15.cloned.1.call-start = ((), (), s32[]{:S(2)}) async-start(), calls=%async_computation.17 | async-start | bytes 10485760 | tf_op jit(solution)/shard_map/reduce_scatter | solution.py:229
  68.6 770.7 %copy-start.55 = (f32[2048]{0:T(1024)}, f32[2048]{0:T(1024)S(1)}, u32[]{:S(2)}) copy-start(f32[2048]{0:T(1024)S(1)} %get-tuple-element.1014) | copy-start | bytes 24580
  68.6 1332.0 %copy-start.48 = (pred[2048]{0:T(1024)(128)(4,1)}, pred[2048]{0:T(1024)(128)(4,1)S(1)}, u32[]{:S(2)}) copy-start(pred[2048]{0:T(1024)(128)(4,1)S(1)} %get-tuple-element.1015) | copy-start | bytes 6148
  68.6 1332.7 %copy-start.50 = (pred[2048]{0:T(1024)(128)(4,1)}, pred[2048]{0:T(1024)(128)(4,1)S(1)}, u32[]{:S(2)}) copy-start(pred[2048]{0:T(1024)(128)(4,1)S(1)} %get-tuple-element.1016) | copy-start | bytes 6148
  851.2 185.4 %all-gather.18.cloned.1.call-start = ((), (), s32[]{:S(2)}) async-start(), calls=%async_computation.19 | async-start | bytes 3244032 | tf_op jit(solution)/shard_map/all_gather | solution.py:196
  853.1 266.3 %all-gather.16.cloned.1.call-start = ((), (), s32[]{:S(2)}) async-start(), calls=%async_computation.18 | async-start | bytes 5242880 | tf_op jit(solution)/shard_map/all_gather | solution.py:236
  998.2 147.5 %all-gather.20.cloned.1.call-start = ((), (), s32[]{:S(2)}) async-start(), calls=%async_computation.20 | async-start | bytes 1622016 | tf_op jit(solution)/shard_map/all_gather | solution.py:197
  999.0 229.1 %all-gather.24.cloned.1.call-start = ((), (), s32[]{:S(2)}) async-start(), calls=%async_computation.29 | async-start | bytes 5242880 | tf_op jit(solution)/shard_map/all_gather | solution.py:203
  1026.2 369.8 %reduce-scatter.19.cloned.1.call-start = ((), (), s32[]{:S(2)}) async-start(), calls=%async_computation.22 | async-start | bytes 10485760 | tf_op jit(solution)/shard_map/reduce_scatter | solution.py:264
  1252.9 229.4 %all-gather.22.cloned.1.call-start = ((), (), s32[]{:S(2)}) async-start(), calls=%async_computation.23 | async-start | bytes 5242880 | tf_op jit(solution)/shard_map/all_gather | solution.py:272
  1400.6 1355.2 %reduce-scatter.21.cloned.1.call-start = ((), (), s32[]{:S(2)}) async-start(), calls=%async_computation.24 | async-start | bytes 5242880 | tf_op jit(solution)/shard_map/reduce_scatter | solution.py:288
  2680.3 155.0 %reduce-scatter.17.cloned.1.call-start = ((), (), s32[]{:S(2)}) async-start(), calls=%async_computation.21 | async-start | bytes 5242880 | tf_op jit(solution)/shard_map/reduce_scatter | solution.py:248
  2688.6 184.8 %reduce-scatter.33.cloned.1.call-start = ((), (), s32[]{:S(2)}) async-start(), calls=%async_computation.31 | async-start | bytes 294912
  2690.3 221.8 %reduce-scatter.31.cloned.1.call-start = ((), (), s32[]{:S(2)}) async-start(), calls=%async_computation.30 | async-start | bytes 589824
  2694.7 261.8 %reduce-scatter.25.cloned.1.call-start = ((), (), s32[]{:S(2)}) async-start(), calls=%async_computation.26 | async-start | bytes 2359296 | tf_op jit(solution)/shard_map/reduce_scatter | solution.py:303
  2700.6 321.9 %reduce-scatter.23.cloned.1.call-start = ((), (), s32[]{:S(2)}) async-start(), calls=%async_computation.25 | async-start | bytes 7077888 | tf_op jit(solution)/shard_map/reduce_scatter | solution.py:300
  2713.6 357.6 %reduce-scatter.29.cloned.1.call-start = ((), (), s32[]{:S(2)}) async-start(), calls=%async_computation.28 | async-start | bytes 3244032 | tf_op jit(solution)/shard_map/reduce_scatter | solution.py:305
  2721.5 413.0 %reduce-scatter.27.cloned.1.call-start = ((), (), s32[]{:S(2)}) async-start(), calls=%async_computation.27 | async-start | bytes 6488064 | tf_op jit(solution)/shard_map/reduce_scatter | solution.py:304
  2842.0 19.1 all-to-all-start.3
  2861.1 140.0 %all-to-all-start.1 = ((bf16[8,64,1024]{2,1,0:T(8,128)(2,1)}), bf16[8,64,1024]{2,1,0:T(8,128)(2,1)S(1)}, u32[]{:S(2)}, u32[]{:S(2)}) async-start(bf16[8,64,1024]{2,1,0:T(8,128)(2,1)} %bitcast.548), calls=%async_computation.3 | async-start | bytes 2097152 | tf_op jit(solution)/shard_map/all_to_all | solution.py:318
  (125 other events, 4089.7 us)
Sparse Core Ops, SparseCore 0:
  10.5 40.4 all-gather.11
  53.2 80.7 all-gather.9
  136.5 22.0 all-gather.13
  851.3 142.8 reduce-scatter.14
  996.5 40.0 all-gather.17
  1038.6 80.7 all-gather.15
  1121.9 23.8 all-gather.19
  1147.3 80.7 all-gather.23
  1253.0 142.9 reduce-scatter.18
  1400.7 81.5 all-gather.21
  2680.5 75.2 reduce-scatter.20
  2758.0 77.2 reduce-scatter.16
  2838.9 34.4 reduce-scatter.32
  2877.2 34.8 reduce-scatter.30
  2915.2 41.1 reduce-scatter.24
  2960.1 62.3 reduce-scatter.22
  3026.3 44.8 reduce-scatter.28
  3075.4 59.0 reduce-scatter.26
where the time goes:
time: 3170 us; the launch traced here: 3140 us
  other arithmetic  978 us (31%)
  waiting for transfers between devices  951 us (30%)
  matrix products  627 us (20%)
  local copies, waits for them, and re-layouts  469 us (15%)
  blocking collectives  78.5 us (2%)
    another operation x256, other arithmetic, one_block(): jax.scipy.linalg.solve_triangular(lower_part, right_side, lower=True, uni...  638 us
    squeeze x256, local copies, waits for them, and re-layouts, delta_blocks(): outputs = lax.scan(jax.checkpoint(one_block), initial, block_items)[1]  187 us
    reduce_scatter x1, waiting for transfers between devices, body(): lax.psum_scatter(jnp.einsum('tcf,dcf->td', grad_pair, ffn_all, preferred_...  143 us
    reduce_scatter x1, waiting for transfers between devices, body(): lax.psum_scatter(jnp.einsum('thv,dhv->td', gated_out, out_all, preferred_...  141 us
    dot_general x128, matrix products, one_block(): jnp.einsum('ihk,jhk->hij', query_rows, block_of_keys, precision=highest_p...  109 us
    dot_general x128, matrix products, one_block(): jnp.einsum('grm,rmj->rgj', block_of_keys, recurrent_matrix, precision=hig...  101 us
    dot_general x128, matrix products, one_block(): jnp.einsum('grm,rmj->rgj', query_rows, recurrent_matrix, precision=highes...  95.9 us
    all_gather x1, waiting for transfers between devices, body(): lax.all_gather(normed_mid_f32.astype(jnp.bfloat16), 'tensor', axis=0, til...  82.8 us
  transfers between devices with their start and end apart: 21, of which 18 were waited for; matrix products, arithmetic and copies ran while one was open for 27% of the time, Pallas kernels for 0%

commit v1 on v0

--- a/solution.py
+++ b/solution.py
@@ -9,6 +9,28 @@
 SEQS = 3
 highest_precision = lax.Precision.HIGHEST
 epsilon = 1e-06
+
+
+def laid_out(tiles, dim):
+    tiles = jnp.moveaxis(tiles, 0, dim)
+    lengths = tiles.shape
+    return tiles.reshape(*lengths[:dim], lengths[dim] * lengths[dim + 1], *lengths[dim + 2 :])
+
+
+def grow_blocks(shard, axis):
+    size = lax.axis_size(axis)
+    pieces = shard[None]
+    for level in range(size.bit_length() - 1):
+        distance = 1 << level
+        received = lax.ppermute(pieces, axis, [(i, i ^ distance) for i in range(size)])
+        both = jnp.stack([pieces, received])
+        upper = lax.axis_index(axis) >> level & 1
+        pieces = jnp.where(upper == 0, both, both[::-1]).reshape(-1, *shard.shape)
+    return pieces
+
+
+def doubled_up(shard, axis, dim):
+    return laid_out(grow_blocks(shard, axis), dim)
 
 
 def rms_scale(values):
@@ -200,7 +222,7 @@
     normed_f32, norm_attn_back = jax.vjp(norm_rows, input_f32, gain_attn)
     normed_all, grad_all = (
         lax.all_gather(normed_f32.astype(jnp.bfloat16), "tensor", axis=0, tiled=True),
-        lax.all_gather(packed_grad, "tensor", axis=0, tiled=True),
+        doubled_up(packed_grad, "tensor", 0),
     )
     projected = jnp.einsum("td,dhp->thp", normed_all, mix_all, preferred_element_type=jnp.float32)
     small_proj = jnp.einsum(

time: 3170 us -> 3170 us (level)
    ppermute x0 -> x2, waiting for transfers between devices: none -> 174 us  [grow_blocks(): lax.ppermute(pieces, axis, [(i, i ^ distance) for i in range(size)])]
    all_gather x1, waiting for transfers between devices: 82.8 us -> 0.01 us  [body(): lax.all_gather(normed_mid_f32.astype(jnp.bfloat16), 'tensor', axis=0, til...]
    all_gather x1 -> x0, waiting for transfers between devices: 82.4 us -> none  [body(): lax.all_gather(packed_grad, 'tensor', axis=0, tiled=True)]
  transfers between devices with their start and end apart: 21 -> 22, of which waited for: 18 -> 16; matrix products, arithmetic and copies ran while one was open for 27% -> 27% of each run, Pallas kernels for 0% -> 0%
where the time goes in v1:
time: 3170 us; the launch traced here: 3140 us
  other arithmetic  988 us (31%)
  waiting for transfers between devices  932 us (29%)
  matrix products  633 us (20%)
  local copies, waits for them, and re-layouts  468 us (15%)
  blocking collectives  79.7 us (3%)
    another operation x256, other arithmetic, one_block(): jax.scipy.linalg.solve_triangular(lower_part, right_side, lower=True, uni...  638 us
    squeeze x256, local copies, waits for them, and re-layouts, delta_blocks(): outputs = lax.scan(jax.checkpoint(one_block), initial, block_items)[1]  187 us
    ppermute x2, waiting for transfers between devices, grow_blocks(): lax.ppermute(pieces, axis, [(i, i ^ distance) for i in range(size)])  174 us
    reduce_scatter x1, waiting for transfers between devices, body(): lax.psum_scatter(jnp.einsum('tcf,dcf->td', grad_pair, ffn_all, preferred_...  143 us
    reduce_scatter x1, waiting for transfers between devices, body(): lax.psum_scatter(jnp.einsum('thv,dhv->td', gated_out, out_all, preferred_...  141 us
    dot_general x128, matrix products, one_block(): jnp.einsum('ihk,jhk->hij', query_rows, block_of_keys, precision=highest_p...  110 us
    dot_general x128, matrix products, one_block(): jnp.einsum('grm,rmj->rgj', block_of_keys, recurrent_matrix, precision=hig...  101 us
    dot_general x128, matrix products, one_block(): jnp.einsum('grm,rmj->rgj', query_rows, recurrent_matrix, precision=highes...  95.8 us
  transfers between devices with their start and end apart: 22, of which 16 were waited for; matrix products, arithmetic and copies ran while one was open for 27% of the time, Pallas kernels for 0%

profile of v1, /device:TPU:0, one launch (start us, length us, event | category | flops | bytes accessed | tf_op | source)
XLA Modules:
  0.0 3143.6 jit_solution(2965207253680491424)
XLA Ops:
  68.6 68.5 %all-gather.8.cloned.1.call-done = bf16[2048,1024]{1,0:T(8,128)(2,1)} async-done(((bf16[512,1024]{1,0:T(8,128)(2,1)}), bf16[2048,1024]{1,0:T(8,128)(2,1)}) %all-gather.8.cloned.1.call-update) | async-done | bytes 4194320 | tf_op jit(solution)/shard_map/all_gather | solution.py:224
  160.8 14.5 fusion.136
  195.3 641.2 %while.41 = (s32[]{:T(128)}, f32[2,128,256]{2,1,0:T(8,128)S(1)}, f32[32,64,2,256]{3,1,2,0:T(8,128)}, f32[32,2,128,256]{3,2,1,0:T(8,128)}, s32[32,64]{1,0:T(8,128...) while((s32[]{:T(128)}, f32[2,128,256]{2,1,0:T(8,128)S(1)}, ...), condition=%wide.region_10.12_spmd.clone, body=%wide.region_8.11_spmd.clone.sunk | while | flops 227238144 | bytes 3428001 | solution.py:160
  856.8 141.0 %reduce-scatter.15.cloned.1.call-done = f32[512,1024]{1,0:T(8,128)} async-done(((f32[2048,1024]{1,0:T(8,128)}), f32[512,1024]{1,0:T(8,128)}) %reduce-scatter.15.cloned.1.call-update) | async-done | bytes 2097168 | tf_op jit(solution)/shard_map/reduce_scatter | solution.py:251
  1004.4 22.6 all_to_all.20
  1031.2 23.7 collective-permute-done
  1062.5 150.0 %collective-permute-done.1 = bf16[2,512,1024]{2,1,0:T(8,128)(2,1)} collective-permute-done((bf16[2,512,1024]{2,1,0:T(8,128)(2,1)}, bf16[2,512,1024]{2,1,0:T(8,128)(2,1)}, u32[]{:S(2)}, u32[]{:S(2)}) %collective-permute-start.1) | collective-permute-done | bytes 2097184 | tf_op jit(solution)/shard_map/ppermute | solution.py:25
  1218.3 11.9 fusion.153
  1253.4 143.4 %reduce-scatter.19.cloned.1.call-done = f32[512,1024]{1,0:T(8,128)} async-done(((f32[2048,1024]{1,0:T(8,128)}), f32[512,1024]{1,0:T(8,128)}) %reduce-scatter.19.cloned.1.call-update) | async-done | bytes 2097168 | tf_op jit(solution)/shard_map/reduce_scatter | solution.py:286
  1403.9 79.7 %all-gather.20.cloned.1.call-done = bf16[2048,1024]{1,0:T(8,128)(2,1)} async-done(((bf16[512,1024]{1,0:T(8,128)(2,1)}), bf16[2048,1024]{1,0:T(8,128)(2,1)}) %all-gather.20.cloned.1.call-update) | async-done | bytes 4194320 | tf_op jit(solution)/shard_map/all_gather | solution.py:294
  1503.4 1110.1 %while.42 = (s32[]{:T(128)}, f32[2,128,256]{2,1,0:T(8,128)}, f32[32,64,2,128]{3,1,0,2:T(8,128)}, f32[32,64,2,128]{3,1,0,2:T(8,128)S(1)}, f32[32,64,2,256]{3,1,0,...) while((s32[]{:T(128)}, f32[2,128,256]{2,1,0:T(8,128)}, ...), condition=%wide.region_29.31_spmd.clone, body=%wide.region_19.30_spmd.clone.sunk | while | flops 612151424 | bytes 10787363 | solution.py:160
  2627.9 16.1 multiply_reduce_fusion.8
  2655.6 13.7 multiply_add_fusion
  2706.4 13.3 fusion.156
  2730.6 12.0 fusion.151
  2743.3 14.6 reduce-scatter.21.cloned.1.call-done
  2760.1 77.5 %reduce-scatter.17.cloned.1.call-done = bf16[512,1024]{1,0:T(8,128)(2,1)} async-done(((bf16[2048,1024]{1,0:T(8,128)(2,1)}), bf16[512,1024]{1,0:T(8,128)(2,1)}) %reduce-scatter.17.cloned.1.call-update) | async-done | bytes 1048592 | tf_op jit(solution)/shard_map/reduce_scatter | solution.py:270
  2850.7 12.6 all-to-all-done.3
  2877.3 37.2 %reduce-scatter.31.cloned.1.call-done = f32[128,4]{1,0:T(8,128)} async-done(((f32[1024,4]{1,0:T(8,128)}), f32[128,4]{1,0:T(8,128)}) %reduce-scatter.31.cloned.1.call-update) | async-done | bytes 2064
  2916.0 42.9 %reduce-scatter.25.cloned.1.call-done = f32[128,2,256]{2,0,1:T(8,128)} async-done(((f32[1024,2,256]{2,0,1:T(8,128)}), f32[128,2,256]{2,0,1:T(8,128)}) %reduce-scatter.25.cloned.1.call-update) | async-done | bytes 262160 | tf_op jit(solution)/shard_map/reduce_scatter | solution.py:325
  2960.7 39.9 %all-reduce.23 = (f32[1024]{0:T(1024)}, f32[1024]{0:T(1024)}, f32[256]{0:T(256)}, f32[8]{0:T(128)}, f32[8]{0:T(128)}) all-reduce(f32[1024]{0:T(1024)S(1)} %get-tuple-element.900, f32[1024]{0:T(1024)S(1)} %copy-done.62, f32[256]{0:T(256)S(1)} %copy-done.78, ...), channel_id=1, replica_groups=mesh['dp'=8,'tensor'=4] {'dp','tensor'}, use_global_device_ids=true, to_apply=%region_45.47 | all-reduce | flops 2320 | bytes 18560 | tf_op jit(solution)/shard_map/psum | solution.py:336
  3006.1 18.7 reduce-scatter.23.cloned.1.call-done
  3027.5 46.1 %reduce-scatter.29.cloned.1.call-done = f32[128,704]{0,1:T(8,128)} async-done(((f32[1024,704]{0,1:T(8,128)}), f32[128,704]{0,1:T(8,128)}) %reduce-scatter.29.cloned.1.call-update) | async-done | bytes 360464 | tf_op jit(solution)/shard_map/reduce_scatter | solution.py:327
  3073.5 63.3 %reduce-scatter.27.cloned.1.call-done = f32[128,2,704]{0,2,1:T(8,128)} async-done(((f32[1024,2,704]{0,2,1:T(8,128)}), f32[128,2,704]{0,2,1:T(8,128)}) %reduce-scatter.27.cloned.1.call-update) | async-done | bytes 720912 | tf_op jit(solution)/shard_map/reduce_scatter | solution.py:326
  (2958 shorter events, 2055.7 us)
Async XLA Ops:
  7.2 61.4 %all-gather.10.cloned.1.call-start = ((), (), s32[]{:S(2)}) async-start(), calls=%async_computation.15 | async-start | bytes 3538944 | tf_op jit(solution)/shard_map/all_gather | solution.py:214
  16.5 23.3 all-to-all-start
  21.7 115.5 %all-gather.8.cloned.1.call-start = ((), (), s32[]{:S(2)}) async-start(), calls=%async_computation.14 | async-start | bytes 5242880 | tf_op jit(solution)/shard_map/all_gather | solution.py:224
  43.6 803.7 %all-gather.12.cloned.1.call-start = ((), (), s32[]{:S(2)}) async-start(), calls=%async_computation.16 | async-start | bytes 1179648 | tf_op jit(solution)/shard_map/all_gather | solution.py:217
  44.4 953.5 %reduce-scatter.15.cloned.1.call-start = ((), (), s32[]{:S(2)}) async-start(), calls=%async_computation.17 | async-start | bytes 10485760 | tf_op jit(solution)/shard_map/reduce_scatter | solution.py:251
  68.6 1334.6 %copy-start.52 = (pred[2048]{0:T(1024)(128)(4,1)}, pred[2048]{0:T(1024)(128)(4,1)S(1)}, u32[]{:S(2)}) copy-start(pred[2048]{0:T(1024)(128)(4,1)S(1)} %get-tuple-element.1018) | copy-start | bytes 6148
  68.6 1415.0 %copy-start.54 = (f32[2048]{0:T(1024)}, f32[2048]{0:T(1024)S(1)}, u32[]{:S(2)}) copy-start(f32[2048]{0:T(1024)S(1)} %get-tuple-element.1015) | copy-start | bytes 24580
  854.8 363.4 %all-gather.16.cloned.1.call-start = ((), (), s32[]{:S(2)}) async-start(), calls=%async_computation.19 | async-start | bytes 3244032 | tf_op jit(solution)/shard_map/all_gather | solution.py:218
  856.7 361.6 %all-gather.14.cloned.1.call-start = ((), (), s32[]{:S(2)}) async-start(), calls=%async_computation.18 | async-start | bytes 5242880 | tf_op jit(solution)/shard_map/all_gather | solution.py:258
  1001.5 228.7 %all-gather.18.cloned.1.call-start = ((), (), s32[]{:S(2)}) async-start(), calls=%async_computation.20 | async-start | bytes 1622016 | tf_op jit(solution)/shard_map/all_gather | solution.py:219
  1029.8 25.1 collective-permute-start
  1059.2 153.2 %collective-permute-start.1 = (bf16[2,512,1024]{2,1,0:T(8,128)(2,1)}, bf16[2,512,1024]{2,1,0:T(8,128)(2,1)}, u32[]{:S(2)}, u32[]{:S(2)}) collective-permute-start(bf16[2,512,1024]{2,1,0:T(8,128)(2,1)} %get-tuple-element.1007), channel_id=1, source_target_pairs={{0,2},{1,3},{2,0},{3,1},{4,6},{5,7},{6,4},{7,5},{8,10},{9,11},{10,... | collective-permute-start | bytes 6291464 | tf_op jit(solution)/shard_map/ppermute | solution.py:25
  1062.4 334.4 %reduce-scatter.19.cloned.1.call-start = ((), (), s32[]{:S(2)}) async-start(), calls=%async_computation.22 | async-start | bytes 10485760 | tf_op jit(solution)/shard_map/reduce_scatter | solution.py:286
  1253.3 230.2 %all-gather.20.cloned.1.call-start = ((), (), s32[]{:S(2)}) async-start(), calls=%async_computation.23 | async-start | bytes 5242880 | tf_op jit(solution)/shard_map/all_gather | solution.py:294
  1401.9 1356.0 %reduce-scatter.21.cloned.1.call-start = ((), (), s32[]{:S(2)}) async-start(), calls=%async_computation.24 | async-start | bytes 5242880 | tf_op jit(solution)/shard_map/reduce_scatter | solution.py:310
  2682.5 155.2 %reduce-scatter.17.cloned.1.call-start = ((), (), s32[]{:S(2)}) async-start(), calls=%async_computation.21 | async-start | bytes 5242880 | tf_op jit(solution)/shard_map/reduce_scatter | solution.py:270
  2694.6 181.1 %reduce-scatter.33.cloned.1.call-start = ((), (), s32[]{:S(2)}) async-start(), calls=%async_computation.30 | async-start | bytes 294912
  2696.3 218.2 %reduce-scatter.31.cloned.1.call-start = ((), (), s32[]{:S(2)}) async-start(), calls=%async_computation.29 | async-start | bytes 589824
  2700.2 258.6 %reduce-scatter.25.cloned.1.call-start = ((), (), s32[]{:S(2)}) async-start(), calls=%async_computation.26 | async-start | bytes 2359296 | tf_op jit(solution)/shard_map/reduce_scatter | solution.py:325
  2706.3 318.5 %reduce-scatter.23.cloned.1.call-start = ((), (), s32[]{:S(2)}) async-start(), calls=%async_computation.25 | async-start | bytes 7077888 | tf_op jit(solution)/shard_map/reduce_scatter | solution.py:322
  2719.7 353.9 %reduce-scatter.29.cloned.1.call-start = ((), (), s32[]{:S(2)}) async-start(), calls=%async_computation.28 | async-start | bytes 3244032 | tf_op jit(solution)/shard_map/reduce_scatter | solution.py:327
  2730.5 406.3 %reduce-scatter.27.cloned.1.call-start = ((), (), s32[]{:S(2)}) async-start(), calls=%async_computation.27 | async-start | bytes 6488064 | tf_op jit(solution)/shard_map/reduce_scatter | solution.py:326
  2844.2 19.1 all-to-all-start.3
  2863.3 140.1 %all-to-all-start.1 = ((bf16[8,64,1024]{2,1,0:T(8,128)(2,1)}), bf16[8,64,1024]{2,1,0:T(8,128)(2,1)S(1)}, u32[]{:S(2)}, u32[]{:S(2)}) async-start(bf16[8,64,1024]{2,1,0:T(8,128)(2,1)} %bitcast.575), calls=%async_computation.3 | async-start | bytes 2097152 | tf_op jit(solution)/shard_map/all_to_all | solution.py:340
  (119 other events, 5932.6 us)
Sparse Core Ops, SparseCore 0:
  10.5 43.6 all-gather.9
  56.4 80.7 all-gather.7
  139.7 22.0 all-gather.11
  854.9 142.8 reduce-scatter.14
  1000.1 40.2 all-gather.15
  1042.5 157.1 all-gather.13
  1202.1 23.1 all-gather.17
  1253.4 143.2 reduce-scatter.18
  1402.0 81.5 all-gather.19
  2682.6 75.2 reduce-scatter.20
  2760.3 77.2 reduce-scatter.16
  2841.1 34.5 reduce-scatter.32
  2879.6 34.7 reduce-scatter.30
  2917.6 41.1 reduce-scatter.24
  2962.4 62.3 reduce-scatter.22
  3028.6 44.8 reduce-scatter.28
  3077.8 58.9 reduce-scatter.26
